TPU v7x, 32 devices: a whole 2x2x4 slice. The times are simulated.
32 devices in a mesh: ctx: 16 (over z, y, x), tp: 2 (over core).
Axes of the slice: x: 2, y: 2, z: 4, core: 2. Of those that a mesh axis runs over, the one named last changes fastest.
Arguments:
- queries: bfloat16 [4096, 2048], P('tp', 'ctx'), may hold values from -6 to 6
- keys_in: bfloat16 [4096, 2048], P('tp', 'ctx'), may hold values from -6 to 6
- values_in: bfloat16 [4096, 2048], P('tp', 'ctx'), may hold values from -6 to 6
- grad_out: bfloat16 [4096, 2048], P('tp', 'ctx'), may hold values from -6 to 6
- residue: float32 [64, 16], replicated, may hold values from -0.07 to 0.07
- decay_rate: float32 [64, 16], replicated, may hold values from 9.765625e-05 to 0.0333333333
Outputs:
- grad_queries: bfloat16 [4096, 2048], P('tp', 'ctx')
- grad_keys: bfloat16 [4096, 2048], P('tp', 'ctx')
- grad_values: bfloat16 [4096, 2048], P('tp', 'ctx')
- grad_residue: float32 [64, 16], replicated
- grad_decay: float32 [64, 16], replicated
All inputs are finite; a program needn't handle non-finite values.
Results may differ from a plain program's by a relative error of at most 0.0085.
Values may be sent and summed in bfloat16 or wider, within the bound.
No kernel may reach another device: no remote copies, remote signals or barrier semaphores. Data moves between devices by JAX's collectives and lax.ppermute only.
A program may use at most 128 MiB of HBM per device.

v0:
```python
import math
import jax
import jax.numpy as jnp
from jax import lax
from jax.sharding import PartitionSpec as P


def dft_tables(size_a, size_b):
    total = size_a * size_b
    rows_a = jnp.arange(size_a, dtype=jnp.int32)
    rows_b = jnp.arange(size_b, dtype=jnp.int32)
    phase_a = (rows_a[:, None] * rows_a[None, :] % size_a).astype(jnp.float32) * (
        2.0 * math.pi / size_a
    )
    phase_b = (rows_b[:, None] * rows_b[None, :] % size_b).astype(jnp.float32) * (
        2.0 * math.pi / size_b
    )
    phase_turn = (rows_a[:, None] * rows_b[None, :] % total).astype(jnp.float32) * (
        2.0 * math.pi / total
    )
    fb_re = jnp.cos(phase_b)
    fb_im = -jnp.sin(phase_b)
    fa_pair = jnp.stack([jnp.cos(phase_a), -jnp.sin(phase_a)], axis=0)
    forward_b = jnp.stack([jnp.stack([fb_re, fb_im], 0), jnp.stack([-fb_im, fb_re], 0)], 0)
    inverse_b = jnp.stack([jnp.stack([fb_re, -fb_im], 0), jnp.stack([fb_im, fb_re], 0)], 0)
    return (fa_pair, forward_b, inverse_b, jnp.cos(phase_turn), -jnp.sin(phase_turn))


def forward_dft(signal, tables):
    fa_pair, forward_b, inverse_b, turn_re, turn_im = tables
    highest = lax.Precision.HIGHEST
    first = jnp.einsum("cab,pak->cpkb", signal, fa_pair, precision=highest)
    first_re = first[:, 0]
    first_im = first[:, 1]
    turned = jnp.stack(
        [
            first_re * turn_re[None] - first_im * turn_im[None],
            first_re * turn_im[None] + first_im * turn_re[None],
        ],
        axis=1,
    )
    return jnp.einsum("cpkb,pqbm->cqkm", turned, forward_b, precision=highest)


def inverse_real(spectrum, tables):
    fa_pair, forward_b, inverse_b, turn_re, turn_im = tables
    highest = lax.Precision.HIGHEST
    middle = jnp.einsum("cpkm,pqbm->cqkb", spectrum, inverse_b, precision=highest)
    middle_re = middle[:, 0]
    middle_im = middle[:, 1]
    back = jnp.stack(
        [
            middle_re * turn_re[None] + middle_im * turn_im[None],
            middle_im * turn_re[None] - middle_re * turn_im[None],
        ],
        axis=1,
    )
    result = jnp.einsum("cpkb,pak->cab", back, fa_pair, precision=highest)
    total = result.shape[1] * result.shape[2]
    return result.reshape(result.shape[0], total) / total


def spectral_work(gated, conv_grad, res_chan, dec_chan):
    chans, length = gated.shape
    total = 2 * length
    size_a = math.isqrt(total)
    while total % size_a != 0:
        size_a -= 1
    size_b = total // size_a
    tables = dft_tables(size_a, size_b)
    highest = lax.Precision.HIGHEST
    positions = jnp.arange(length).astype(jnp.float32)
    basis = jnp.exp(-dec_chan[:, :, None] * positions[None, None, :])
    filt = jnp.einsum("cm,cmt->ct", res_chan, basis, precision=highest)
    fields = jnp.concatenate(
        [gated.astype(jnp.float32), filt, conv_grad.astype(jnp.float32)], axis=0
    )
    padded = jnp.concatenate([fields, jnp.zeros((3 * chans, length), jnp.float32)], axis=1)
    spectra = forward_dft(padded.reshape(3 * chans, size_a, size_b), tables)
    gated_re = spectra[:chans, 0]
    gated_im = spectra[:chans, 1]
    filt_re = spectra[chans : 2 * chans, 0]
    filt_im = spectra[chans : 2 * chans, 1]
    cot_re = spectra[2 * chans :, 0]
    cot_im = spectra[2 * chans :, 1]
    products_re = jnp.concatenate(
        [
            gated_re * filt_re - gated_im * filt_im,
            filt_re * cot_re + filt_im * cot_im,
            gated_re * cot_re + gated_im * cot_im,
        ],
        axis=0,
    )
    products_im = jnp.concatenate(
        [
            gated_re * filt_im + gated_im * filt_re,
            filt_re * cot_im - filt_im * cot_re,
            gated_re * cot_im - gated_im * cot_re,
        ],
        axis=0,
    )
    results = inverse_real(jnp.stack([products_re, products_im], axis=1), tables)[:, :length]
    conv = results[:chans].astype(jnp.bfloat16)
    input_grad = results[chans : 2 * chans].astype(jnp.bfloat16)
    filter_grad = results[2 * chans :]
    res_terms = jnp.einsum("ct,cmt->cm", filter_grad, basis, precision=highest)
    dec_terms = (
        -res_chan
        * dec_chan
        * jnp.einsum("ct,cmt->cm", filter_grad * positions[None, :], basis, precision=highest)
    )
    return (conv, input_grad, res_terms, dec_terms)


def product_bf(first, second):
    return (first.astype(jnp.float32) * second.astype(jnp.float32)).astype(jnp.bfloat16)


def per_device(queries, keys_in, values_in, grad_out, residue, decay_rate):
    chans_tp, tokens_dev = queries.shape
    ctx_count = lax.axis_size("ctx")
    groups_count = residue.shape[0]
    highest = lax.Precision.HIGHEST
    chans_dev = chans_tp // ctx_count
    channel_ids = (
        lax.axis_index("tp") * chans_tp
        + lax.axis_index("ctx") * chans_dev
        + jnp.arange(chans_dev, dtype=jnp.int32)
    )
    onehot = (
        (channel_ids % groups_count)[:, None] == jnp.arange(groups_count, dtype=jnp.int32)[None, :]
    ).astype(jnp.float32)
    res_chan = jnp.dot(onehot, residue, precision=highest)
    dec_chan = jnp.dot(onehot, decay_rate, precision=highest)

    def to_blocks(field):
        return field.reshape(ctx_count, chans_dev, tokens_dev)

    def to_whole(field):
        return field.reshape(chans_dev, ctx_count * tokens_dev)

    def to_return(field):
        return field.reshape(1, chans_dev, ctx_count * tokens_dev)

    moved_query, moved_key, moved_value, moved_grad = (
        lax.all_to_all(to_blocks(queries), "ctx", split_axis=0, concat_axis=2, tiled=True),
        lax.all_to_all(to_blocks(keys_in), "ctx", split_axis=0, concat_axis=2, tiled=True),
        lax.all_to_all(to_blocks(values_in), "ctx", split_axis=0, concat_axis=2, tiled=True),
        lax.all_to_all(to_blocks(grad_out), "ctx", split_axis=0, concat_axis=2, tiled=True),
    )
    whole_query = to_whole(moved_query)
    whole_key = to_whole(moved_key)
    whole_value = to_whole(moved_value)
    whole_grad = to_whole(moved_grad)
    gated = product_bf(whole_key, whole_value)
    conv_grad = product_bf(whole_grad, whole_query)
    conv, input_grad, res_terms, dec_terms = spectral_work(gated, conv_grad, res_chan, dec_chan)
    grad_q_ch = product_bf(whole_grad, conv)
    grad_k_ch = product_bf(input_grad, whole_value)
    grad_v_ch = product_bf(input_grad, whole_key)
    back_q, back_k, back_v = (
        lax.all_to_all(to_return(grad_q_ch), "ctx", split_axis=2, concat_axis=0, tiled=True),
        lax.all_to_all(to_return(grad_k_ch), "ctx", split_axis=2, concat_axis=0, tiled=True),
        lax.all_to_all(to_return(grad_v_ch), "ctx", split_axis=2, concat_axis=0, tiled=True),
    )
    grad_queries = back_q.reshape(chans_tp, tokens_dev)
    grad_keys = back_k.reshape(chans_tp, tokens_dev)
    grad_values = back_v.reshape(chans_tp, tokens_dev)
    res_group = jnp.dot(onehot.T, res_terms, precision=highest)
    dec_group = jnp.dot(onehot.T, dec_terms, precision=highest)
    res_total, dec_total = lax.psum((res_group, dec_group), ("ctx", "tp"))
    whole_length = ctx_count * tokens_dev
    return (
        grad_queries,
        grad_keys,
        grad_values,
        res_total / whole_length,
        dec_total / whole_length,
    )


def solution(mesh):
    in_specs = (P("tp", "ctx"), P("tp", "ctx"), P("tp", "ctx"), P("tp", "ctx"), P(), P())
    out_specs = (P("tp", "ctx"), P("tp", "ctx"), P("tp", "ctx"), P(), P())
    return jax.shard_map(
        per_device, mesh=mesh, in_specs=in_specs, out_specs=out_specs, check_vma=False
    )
```

profile of v0, /device:TPU:0, one launch (start us, length us, event | category | flops | bytes accessed | tf_op | source)
XLA Modules:
  0.0 373.3 jit_solution(8923494113238331859)
XLA Ops:
  0.6 23.4 %all_to_all.81 = bf16[16,128,128]{2,1,0:T(8,128)(2,1)S(1)} all-to-all(bf16[16,128,128]{2,1,0:T(8,128)(2,1)} %bitcast.183), channel_id=1, replica_groups=mesh['ctx'=16,'tp'=2] {'ctx'}, dimensions={0} | all-to-all | bytes 1048576 | tf_op jit(solution)/shard_map/all_to_all | solution.py:147
  24.1 3.9 %all-to-all-start.2 = ((bf16[16,128,128]{2,1,0:T(8,128)(2,1)}), bf16[16,128,128]{2,1,0:T(8,128)(2,1)S(1)}, u32[]{:S(2)}, u32[]{:S(2)}) async-start(bf16[16,128,128]{2,1,0:T(8,128)(2,1)} %bitcast.184), calls=%async_computation.2 | async-start | bytes 1048576 | tf_op jit(solution)/shard_map/all_to_all | solution.py:148
  29.1 13.3 %all-to-all-done.2 = bf16[16,128,128]{2,1,0:T(8,128)(2,1)S(1)} async-done(((bf16[16,128,128]{2,1,0:T(8,128)(2,1)}), bf16[16,128,128]{2,1,0:T(8,128)(2,1)S(1)}, u32[]{:S(2)}, u32[]{:S(2)}) %all-to-all-start.2) | async-done | bytes 524320 | tf_op jit(solution)/shard_map/all_to_all | solution.py:148
  42.5 3.9 %all-to-all-start.3 = ((bf16[16,128,128]{2,1,0:T(8,128)(2,1)}), bf16[16,128,128]{2,1,0:T(8,128)(2,1)S(1)}, u32[]{:S(2)}, u32[]{:S(2)}) async-start(bf16[16,128,128]{2,1,0:T(8,128)(2,1)} %bitcast.185), calls=%async_computation.3 | async-start | bytes 1048576 | tf_op jit(solution)/shard_map/all_to_all | solution.py:146
  47.3 5.1 %multiply_reduce_fusion.1 = f32[128,2048]{1,0:T(8,128)S(1)} fusion(f32[128,16]{1,0:T(8,128)S(1)} %copy.93, f32[2048]{0:T(1024)S(1)} %iota_convert_fusion, f32[128,16]{1,0:T(8,128)S(1)} %copy.49), kind=kLoop, calls=%fused_computation.1 | loop fusion | flops 12320768 | bytes 1073152
  52.5 1.3 copy.69
  54.1 6.6 %all-to-all-done.3 = bf16[16,128,128]{2,1,0:T(8,128)(2,1)S(1)} async-done(((bf16[16,128,128]{2,1,0:T(8,128)(2,1)}), bf16[16,128,128]{2,1,0:T(8,128)(2,1)S(1)}, u32[]{:S(2)}, u32[]{:S(2)}) %all-to-all-start.3) | async-done | bytes 524320 | tf_op jit(solution)/shard_map/all_to_all | solution.py:146
  60.8 4.4 %all-to-all-start = ((bf16[16,128,128]{2,1,0:T(8,128)(2,1)}), bf16[16,128,128]{2,1,0:T(8,128)(2,1)}, u32[]{:S(2)}, u32[]{:S(2)}) async-start(bf16[16,128,128]{2,1,0:T(8,128)(2,1)} %bitcast.1), calls=%async_computation | async-start | bytes 1048576 | tf_op jit(solution)/shard_map/all_to_all | solution.py:149
  65.8 1.5 convert_bitcast_fusion.1
  67.7 1.5 convert_bitcast_fusion
  69.2 1.3 copy.50
  70.5 8.6 %all-to-all-done = bf16[16,128,128]{2,1,0:T(8,128)(2,1)} async-done(((bf16[16,128,128]{2,1,0:T(8,128)(2,1)}), bf16[16,128,128]{2,1,0:T(8,128)(2,1)}, u32[]{:S(2)}, u32[]{:S(2)}) %all-to-all-start) | async-done | bytes 524320 | tf_op jit(solution)/shard_map/all_to_all | solution.py:149
  79.1 2.1 convert_bitcast_fusion.3
  81.3 1.6 copy.46
  82.8 2.0 fusion.33
  85.3 14.2 %fusion.17 = f32[384,2,64,64]{0,2,3,1:T(8,128)S(1)} fusion(f32[384,64,64]{0,2,1:T(8,128)S(1)} %bitcast.170, f32[1,64,64]{1,2,0:T(8,128)S(1)} %get-tuple-element.32, f32[1,64,64]{1,2,0:T(8,128)S(1)} %get-tuple-element.33), kind=kOutput, calls=%fused_computation.33 | convolution fusion | flops 2415927296 | bytes 18907136 | tf_op jit(solution)/shard_map/cab,pak->cpkb/dot_general | solution.py:32
  99.5 3.7 multiply_subtract_fusion.1
  103.3 9.6 %pad_maximum_fusion = f32[384,2,64,64]{0,2,3,1:T(8,128)} fusion(f32[384,1,64,64]{0,2,3,1:T(8,128)} %get-tuple-element.10, f32[384,1,64,64]{0,2,3,1:T(8,128)S(1)} %get-tuple-element.9), kind=kLoop, calls=%fused_computation.4 | loop fusion | flops 3145728 | bytes 25165824 | tf_op jit(solution)/shard_map/stack | solution.py:35
  112.9 22.9 %fusion.20 = f32[384,2,64,64]{0,3,2,1:T(8,128)S(1)} fusion(f32[384,2,64,64]{0,2,3,1:T(8,128)} %pad_maximum_fusion, f32[1,2,64,64]{2,3,1,0:T(8,128)S(1)} %get-tuple-element.23, f32[1,2,64,64]{2,3,1,0:T(8,128)S(1)} %get-tuple-element.26), kind=kOutput, calls=%fused_computation.34 | convolution fusion | flops 4831854592 | bytes 25231360 | tf_op jit(solution)/shard_map/cpkb,pqbm->cqkm/dot_general | solution.py:42
  135.7 2.8 subtract_bitcast_fusion.1
  138.5 4.3 %subtract_bitcast_fusion.2 = (f32[128,64,64]{0,2,1:T(8,128)}, f32[128,64,64]{0,2,1:T(8,128)}, f32[128,64,64]{0,2,1:T(8,128)}, f32[128,64,64]{0,2,1:T(8,128)}) fusion(f32[384,2,64,64]{0,3,2,1:T(8,128)S(1)} %fusion.20), kind=kLoop, calls=%fused_computation.41 | loop fusion | flops 6291456 | bytes 20971520 | tf_op jit(solution)/shard_map/sub | solution.py:88
  142.8 3.7 maximum_bitcast_fusion.1
  148.2 13.7 %fusion.23 = f32[2,64,384,64]{2,1,3,0:T(8,128)} fusion(f32[384,1,64,64]{0,3,2,1:T(8,128)S(1)} %maximum_bitcast_fusion.1, f32[384,1,64,64]{0,3,2,1:T(8,128)S(1)} %maximum_bitcast_fusion, f32[1,2,64,64]{2,3,1,0:T(8,128)S(1)} %get-tuple-element.27, f32[1,2,64,64]{2,3,1,0:T(8,128)S(1)} %get-tuple-element.22), kind=kOutput, calls=%fused_computation.35 | convolution fusion | flops 4835000320 | bytes 25231360 | tf_op jit(solution)/shard_map/cpkm,pqbm->cqkb/dot_general | solution.py:48
  161.9 16.4 %copy.121 = f32[2,64,384,64]{2,3,1,0:T(8,128)} copy(f32[2,64,384,64]{2,1,3,0:T(8,128)} %fusion.23) | data formatting | bytes 25165824 | tf_op jit(solution)/shard_map/cpkm,pqbm->cqkb/dot_general | solution.py:48
  178.3 6.0 %multiply_add_fusion = (f32[384,1,64,64]{0,2,3,1:T(8,128)S(1)}, f32[384,1,64,64]{0,2,3,1:T(8,128)S(1)}) fusion(f32[384,2,64,64]{0,2,3,1:T(8,128)} %bitcast.168, f32[64,64]{0,1:T(8,128)S(1)} %get-tuple-element.34, f32[64,64]{0,1:T(8,128)S(1)} %get-tuple-element.35), kind=kLoop, calls=%fused_computation.30 | loop fusion | flops 9437184 | bytes 25198592 | tf_op jit(solution)/shard_map/add | solution.py:53
  184.3 7.4 %fusion.13 = f32[384,64,64]{0,1,2:T(8,128)S(1)} fusion(f32[384,1,64,64]{0,2,3,1:T(8,128)S(1)} %get-tuple-element.8, f32[384,1,64,64]{0,2,3,1:T(8,128)S(1)} %get-tuple-element.7, f32[1,64,64]{1,2,0:T(8,128)S(1)} %get-tuple-element.32, f32[1,64,64]{1,2,0:T(8,128)S(1)} %get-tuple-element.33), kind=kOutput, calls=%fused_computation.23 | convolution fusion | flops 2420645888 | bytes 18907136 | tf_op jit(solution)/shard_map/cpkb,pak->cab/dot_general | solution.py:58
  191.7 3.6 copy.59
  196.2 1.2 copy-done.4
  197.4 1.1 copy-done.6
  198.5 1.0 copy-done.8
  199.8 8.5 %copy.124 = bf16[1,128,2048]{1,0,2:T(2,128)(2,1)S(1)} copy(bf16[1,128,2048]{1,2,0:T(8,128)(2,1)S(1)} %bitcast.182) | data formatting | bytes 1048576 | tf_op jit(solution)/shard_map/reshape | solution.py:143
  208.9 11.5 %reduce.4 = bf16[2048,128]{1,0:T(8,128)(2,1)S(1)} reduce(bf16[2048,1,128]{2,1,0:T(2,128)(2,1)S(1)} %bitcast.174, bf16[]{:T(256)} %broadcast.254), dimensions={1}, to_apply=%bitcast.167.reduce_sub_computation | reduce | bytes 1048578
  221.3 4.0 %all-to-all-start.4 = ((bf16[16,2,8192]{2,1,0:T(2,128)(2,1)}), bf16[16,2,8192]{2,1,0:T(2,128)(2,1)S(1)}, u32[]{:S(2)}, u32[]{:S(2)}) async-start(bf16[16,2,8192]{2,1,0:T(2,128)(2,1)} %reshape.263), calls=%async_computation.4 | async-start | bytes 1048576 | tf_op jit(solution)/shard_map/all_to_all | solution.py:162
  225.3 8.1 %copy.123 = bf16[1,128,2048]{1,0,2:T(2,128)(2,1)S(1)} copy(bf16[1,128,2048]{1,2,0:T(8,128)(2,1)S(1)} %bitcast.181) | data formatting | bytes 1048576 | tf_op jit(solution)/shard_map/reshape | solution.py:143
  233.5 11.5 %reduce.5 = bf16[2048,128]{1,0:T(8,128)(2,1)S(1)} reduce(bf16[2048,1,128]{2,1,0:T(2,128)(2,1)S(1)} %bitcast.176, bf16[]{:T(256)} %broadcast.254), dimensions={1}, to_apply=%bitcast.166.reduce_sub_computation | reduce | bytes 1048578
  245.9 8.3 %copy.122 = bf16[1,128,2048]{1,0,2:T(2,128)(2,1)S(1)} copy(bf16[1,128,2048]{1,2,0:T(8,128)(2,1)S(1)} %bitcast.180) | data formatting | bytes 1048576 | tf_op jit(solution)/shard_map/reshape | solution.py:143
  254.2 11.5 %reduce.6 = bf16[2048,128]{1,0:T(8,128)(2,1)S(1)} reduce(bf16[2048,1,128]{2,1,0:T(2,128)(2,1)S(1)} %bitcast.175, bf16[]{:T(256)} %broadcast.254), dimensions={1}, to_apply=%bitcast.165.reduce_sub_computation | reduce | bytes 1048578
  266.7 7.0 %all-to-all-start.5 = ((bf16[16,2,8192]{2,1,0:T(2,128)(2,1)}), bf16[16,2,8192]{2,1,0:T(2,128)(2,1)S(1)}, u32[]{:S(2)}, u32[]{:S(2)}) async-start(bf16[16,2,8192]{2,1,0:T(2,128)(2,1)} %reshape.265), calls=%async_computation.5 | async-start | bytes 1048576 | tf_op jit(solution)/shard_map/all_to_all | solution.py:163
  273.7 1.6 slice_multiply_fusion
  275.3 2.0 copy.77
  277.6 3.3 multiply_reduce_fusion
  280.9 6.4 %all-to-all-done.5 = bf16[16,2,8192]{2,1,0:T(2,128)(2,1)S(1)} async-done(((bf16[16,2,8192]{2,1,0:T(2,128)(2,1)}), bf16[16,2,8192]{2,1,0:T(2,128)(2,1)S(1)}, u32[]{:S(2)}, u32[]{:S(2)}) %all-to-all-start.5) | async-done | bytes 524320 | tf_op jit(solution)/shard_map/all_to_all | solution.py:163
  287.3 3.8 %all-to-all-start.6 = ((bf16[16,2,8192]{2,1,0:T(2,128)(2,1)}), bf16[16,2,8192]{2,1,0:T(2,128)(2,1)S(1)}, u32[]{:S(2)}, u32[]{:S(2)}) async-start(bf16[16,2,8192]{2,1,0:T(2,128)(2,1)} %reshape.267), calls=%async_computation.6 | async-start | bytes 1048576 | tf_op jit(solution)/shard_map/all_to_all | solution.py:164
  291.2 34.5 %fusion = f32[128,1,16]{2,1,0:T(1,128)S(1)} fusion(f32[128,2048,1]{1,2,0:T(1,128)S(1)} %copy-done.15, f32[2048]{0:T(1024)S(1)} %iota_convert_fusion, f32[128,16]{1,0:T(8,128)S(1)} %copy-done.17), kind=kOutput, calls=%fused_computation.3 | convolution fusion | flops 54525952 | bytes 1073152 | tf_op jit(solution)/shard_map/ct,cmt->cm/dot_general | solution.py:106
  326.3 40.7 %all-reduce.1 = (f32[64,16]{0,1:T(8,128)S(1)}, f32[64,16]{0,1:T(8,128)S(1)}) all-reduce(f32[64,16]{0,1:T(8,128)S(1)} %fusion.43, f32[64,16]{0,1:T(8,128)S(1)} %fusion.42), channel_id=1, replica_groups=mesh['ctx'=16,'tp'=2] {'ctx','tp'}, use_global_device_ids=true, to_apply=%region_0.1 | all-reduce | flops 2048 | bytes 16384 | tf_op jit(solution)/shard_map/psum | solution.py:171
  368.8 1.0 copy.61
  370.4 1.0 copy.63
  372.1 1.0 copy.65
  (74 shorter events, 13.6 us)
Async XLA Ops:
  0.6 45.7 %copy-start = (f32[64,16]{0,1:T(8,128)S(1)}, f32[64,16]{0,1:T(8,128)}, u32[]{:S(2)}) copy-start(f32[64,16]{0,1:T(8,128)} %param.11) | copy-start | bytes 12292
  24.1 18.4 %all-to-all-start.2 = ((bf16[16,128,128]{2,1,0:T(8,128)(2,1)}), bf16[16,128,128]{2,1,0:T(8,128)(2,1)S(1)}, u32[]{:S(2)}, u32[]{:S(2)}) async-start(bf16[16,128,128]{2,1,0:T(8,128)(2,1)} %bitcast.184), calls=%async_computation.2 | async-start | bytes 1048576 | tf_op jit(solution)/shard_map/all_to_all | solution.py:148
  28.1 37.3 %copy-start.18 = (s32[128]{0:T(128)}, s32[128]{0:T(128)S(1)}, u32[]{:S(2)}) copy-start(s32[128]{0:T(128)S(1)} %and_select_fusion) | copy-start | bytes 1540
  42.5 22.9 %copy-start.13 = (bf16[16,128,128]{2,1,0:T(8,128)(2,1)}, bf16[16,128,128]{2,1,0:T(8,128)(2,1)S(1)}, u32[]{:S(2)}) copy-start(bf16[16,128,128]{2,1,0:T(8,128)(2,1)S(1)} %all-to-all-done.2) | copy-start | bytes 1572868
  42.5 18.3 %all-to-all-start.3 = ((bf16[16,128,128]{2,1,0:T(8,128)(2,1)}), bf16[16,128,128]{2,1,0:T(8,128)(2,1)S(1)}, u32[]{:S(2)}, u32[]{:S(2)}) async-start(bf16[16,128,128]{2,1,0:T(8,128)(2,1)} %bitcast.185), calls=%async_computation.3 | async-start | bytes 1048576 | tf_op jit(solution)/shard_map/all_to_all | solution.py:146
  47.3 18.2 %copy-start.16 = (f32[128,16]{1,0:T(8,128)}, f32[128,16]{1,0:T(8,128)S(1)}, u32[]{:S(2)}) copy-start(f32[128,16]{1,0:T(8,128)S(1)} %copy.49) | copy-start | bytes 24580
  60.8 4.6 %copy-start.14 = (bf16[16,128,128]{2,1,0:T(8,128)(2,1)}, bf16[16,128,128]{2,1,0:T(8,128)(2,1)S(1)}, u32[]{:S(2)}) copy-start(bf16[16,128,128]{2,1,0:T(8,128)(2,1)S(1)} %all-to-all-done.3) | copy-start | bytes 1572868
  60.8 18.4 %all-to-all-start = ((bf16[16,128,128]{2,1,0:T(8,128)(2,1)}), bf16[16,128,128]{2,1,0:T(8,128)(2,1)}, u32[]{:S(2)}, u32[]{:S(2)}) async-start(bf16[16,128,128]{2,1,0:T(8,128)(2,1)} %bitcast.1), calls=%async_computation | async-start | bytes 1048576 | tf_op jit(solution)/shard_map/all_to_all | solution.py:149
  65.8 19.0 %copy-start.3 = (f32[1,128,16,128]{1,3,2,0:T(8,128)}, f32[1,128,16,128]{1,3,2,0:T(8,128)S(1)}, u32[]{:S(2)}) copy-start(f32[1,128,16,128]{1,3,2,0:T(8,128)S(1)} %copy.47) | copy-start | bytes 3145732
  67.7 17.2 %copy-start.5 = (f32[1,128,16,128]{1,3,2,0:T(8,128)}, f32[1,128,16,128]{1,3,2,0:T(8,128)S(1)}, u32[]{:S(2)}) copy-start(f32[1,128,16,128]{1,3,2,0:T(8,128)S(1)} %copy.48) | copy-start | bytes 3145732
  82.8 2.5 copy-start.7
  82.8 2.1 copy-start.12
  142.8 3.7 copy-start.9
  142.8 4.1 %copy-start.10 = (f32[128,64,64]{0,2,1:T(8,128)S(1)}, f32[128,64,64]{0,2,1:T(8,128)}, u32[]{:S(2)}) copy-start(f32[128,64,64]{0,2,1:T(8,128)} %get-tuple-element.12) | copy-start | bytes 6291460
  142.8 4.7 %copy-start.11 = (f32[128,64,64]{0,2,1:T(8,128)S(1)}, f32[128,64,64]{0,2,1:T(8,128)}, u32[]{:S(2)}) copy-start(f32[128,64,64]{0,2,1:T(8,128)} %get-tuple-element.13) | copy-start | bytes 6291460
  195.4 4.4 %copy-start.2 = (f32[384,64,64]{0,2,1:T(8,128)}, f32[384,64,64]{0,2,1:T(8,128)S(1)}, u32[]{:S(2)}) copy-start(f32[384,64,64]{0,2,1:T(8,128)S(1)} %copy.59) | copy-start | bytes 18874372
  195.4 2.0 copy-start.4
  195.4 3.1 copy-start.6
  195.4 4.1 %copy-start.8 = (f32[1,128,16,128]{1,3,2,0:T(8,128)S(1)}, f32[1,128,16,128]{1,3,2,0:T(8,128)}, u32[]{:S(2)}) copy-start(f32[1,128,16,128]{1,3,2,0:T(8,128)} %copy-done.7) | copy-start | bytes 3145732
  221.3 45.4 %all-to-all-start.4 = ((bf16[16,2,8192]{2,1,0:T(2,128)(2,1)}), bf16[16,2,8192]{2,1,0:T(2,128)(2,1)S(1)}, u32[]{:S(2)}, u32[]{:S(2)}) async-start(bf16[16,2,8192]{2,1,0:T(2,128)(2,1)} %reshape.263), calls=%async_computation.4 | async-start | bytes 1048576 | tf_op jit(solution)/shard_map/all_to_all | solution.py:162
  245.9 31.7 %copy-start.17 = (f32[128,16]{1,0:T(8,128)S(1)}, f32[128,16]{1,0:T(8,128)}, u32[]{:S(2)}) copy-start(f32[128,16]{1,0:T(8,128)} %copy-done.16) | copy-start | bytes 24580
  266.7 20.6 %all-to-all-start.5 = ((bf16[16,2,8192]{2,1,0:T(2,128)(2,1)}), bf16[16,2,8192]{2,1,0:T(2,128)(2,1)S(1)}, u32[]{:S(2)}, u32[]{:S(2)}) async-start(bf16[16,2,8192]{2,1,0:T(2,128)(2,1)} %reshape.265), calls=%async_computation.5 | async-start | bytes 1048576 | tf_op jit(solution)/shard_map/all_to_all | solution.py:163
  277.6 13.6 %copy-start.15 = (f32[128,2048,1]{1,2,0:T(1,128)S(1)}, f32[128,2048,1]{1,2,0:T(1,128)}, u32[]{:S(2)}) copy-start(f32[128,2048,1]{1,2,0:T(1,128)} %copy.77) | copy-start | bytes 3145732
  287.3 84.2 %all-to-all-start.6 = ((bf16[16,2,8192]{2,1,0:T(2,128)(2,1)}), bf16[16,2,8192]{2,1,0:T(2,128)(2,1)S(1)}, u32[]{:S(2)}, u32[]{:S(2)}) async-start(bf16[16,2,8192]{2,1,0:T(2,128)(2,1)} %reshape.267), calls=%async_computation.6 | async-start | bytes 1048576 | tf_op jit(solution)/shard_map/all_to_all | solution.py:164
  291.2 34.6 %copy-start.19 = (s32[128]{0:T(128)S(1)}, s32[128]{0:T(128)}, u32[]{:S(2)}) copy-start(s32[128]{0:T(128)} %copy-done.18) | copy-start | bytes 1540
  291.2 34.6 %copy-start.20 = (f32[128,16]{0,1:T(8,128)S(1)}, f32[128,16]{0,1:T(8,128)}, u32[]{:S(2)}) copy-start(f32[128,16]{0,1:T(8,128)} %get-tuple-element.29) | copy-start | bytes 24580
  367.6 5.5 %copy-start.1 = (f32[64,16]{0,1:T(8,128)S(1)}, f32[64,16]{0,1:T(8,128)}, u32[]{:S(2)}) copy-start(f32[64,16]{0,1:T(8,128)} %param.11) | copy-start | bytes 12292
where the time goes:
time: 377 us; the launch traced here: 373 us
  matrix products  95 us (25%)
  other arithmetic  85.7 us (23%)
  local copies, waits for them, and re-layouts  65 us (17%)
  blocking collectives  64.1 us (17%)
  waiting for transfers between devices  35 us (9%)
  starting transfers between devices  27.1 us (7%)
    unnamed x5, other arithmetic  43 us
    psum x1, blocking collectives, per_device(): res_total, dec_total = lax.psum((res_group, dec_group), ('ctx', 'tp'))  40.7 us
    dot_general x1, matrix products, spectral_work(): res_terms = jnp.einsum('ct,cmt->cm', filter_grad, basis, precision=highest)  34.5 us
    reshape x3, local copies, waits for them, and re-layouts, to_return(): return field.reshape(1, chans_dev, ctx_count * tokens_dev)  25 us
    all_to_all x1, blocking collectives, per_device(): lax.all_to_all(to_blocks(keys_in), 'ctx', split_axis=0, concat_axis=2, ti...  23.4 us
    dot_general x1, matrix products, forward_dft(): return jnp.einsum('cpkb,pqbm->cqkm', turned, forward_b, precision=highest)  22.9 us
    dot_general x1, local copies, waits for them, and re-layouts, inverse_real(): jnp.einsum('cpkm,pqbm->cqkb', spectrum, inverse_b, precision=highest)  16.4 us
    dot_general x1, matrix products, forward_dft(): first = jnp.einsum('cab,pak->cpkb', signal, fa_pair, precision=highest)  14.2 us
  transfers between devices with their start and end apart: 6, of which 4 were waited for; matrix products, arithmetic and copies ran while one was open for 27% of the time, Pallas kernels for 0%

commit v1 on v0

--- a/solution.py
+++ b/solution.py
@@ -168,7 +168,7 @@
     grad_values = back_v.reshape(chans_tp, tokens_dev)
     res_group = jnp.dot(onehot.T, res_terms, precision=highest)
     dec_group = jnp.dot(onehot.T, dec_terms, precision=highest)
-    res_total, dec_total = lax.psum((res_group, dec_group), ("ctx", "tp"))
+    res_total, dec_total = lax.psum(lax.psum((res_group, dec_group), "tp"), "ctx")
     whole_length = ctx_count * tokens_dev
     return (
         grad_queries,

time: 377 us -> 417 us (1.11)
  blocking collectives: 64.1 us -> 104 us
    psum x1 -> x2, blocking collectives: 40.7 us -> 80.4 us  [the longest x1 77.1 us: per_device(): lax.psum(lax.psum((res_group, dec_group), 'tp'), 'ctx')]
  transfers between devices with their start and end apart: 6 -> 6, of which waited for: 4 -> 4; matrix products, arithmetic and copies ran while one was open for 27% -> 25% of each run, Pallas kernels for 0% -> 0%
where the time goes in v1:
time: 417 us; the launch traced here: 413 us
  blocking collectives  104 us (25%)
  matrix products  95.1 us (23%)
  other arithmetic  85.7 us (21%)
  local copies, waits for them, and re-layouts  65 us (16%)
  waiting for transfers between devices  35 us (8%)
  starting transfers between devices  27.1 us (6%)
    psum x1, blocking collectives, per_device(): lax.psum(lax.psum((res_group, dec_group), 'tp'), 'ctx')  77.1 us
    unnamed x5, other arithmetic  43 us
    dot_general x1, matrix products, spectral_work(): res_terms = jnp.einsum('ct,cmt->cm', filter_grad, basis, precision=highest)  34.5 us
    reshape x3, local copies, waits for them, and re-layouts, to_return(): return field.reshape(1, chans_dev, ctx_count * tokens_dev)  25 us
    all_to_all x1, blocking collectives, per_device(): lax.all_to_all(to_blocks(keys_in), 'ctx', split_axis=0, concat_axis=2, ti...  23.4 us
    dot_general x1, matrix products, forward_dft(): return jnp.einsum('cpkb,pqbm->cqkm', turned, forward_b, precision=highest)  22.9 us
    dot_general x1, local copies, waits for them, and re-layouts, inverse_real(): jnp.einsum('cpkm,pqbm->cqkb', spectrum, inverse_b, precision=highest)  16.4 us
    dot_general x1, matrix products, forward_dft(): first = jnp.einsum('cab,pak->cpkb', signal, fa_pair, precision=highest)  14.2 us
  transfers between devices with their start and end apart: 6, of which 4 were waited for; matrix products, arithmetic and copies ran while one was open for 25% of the time, Pallas kernels for 0%

profile of v1, /device:TPU:0, one launch (start us, length us, event | category | flops | bytes accessed | tf_op | source)
XLA Modules:
  0.0 413.1 jit_solution(1348056130374348260)
XLA Ops:
  0.6 23.4 %all_to_all.81 = bf16[16,128,128]{2,1,0:T(8,128)(2,1)S(1)} all-to-all(bf16[16,128,128]{2,1,0:T(8,128)(2,1)} %bitcast.183), channel_id=1, replica_groups=mesh['ctx'=16,'tp'=2] {'ctx'}, dimensions={0} | all-to-all | bytes 1048576 | tf_op jit(solution)/shard_map/all_to_all | solution.py:147
  24.1 3.9 all-to-all-start.2
  29.1 13.3 %all-to-all-done.2 = bf16[16,128,128]{2,1,0:T(8,128)(2,1)S(1)} async-done(((bf16[16,128,128]{2,1,0:T(8,128)(2,1)}), bf16[16,128,128]{2,1,0:T(8,128)(2,1)S(1)}, u32[]{:S(2)}, u32[]{:S(2)}) %all-to-all-start.2) | async-done | bytes 524320 | tf_op jit(solution)/shard_map/all_to_all | solution.py:148
  42.5 3.9 all-to-all-start.3
  47.3 5.1 %multiply_reduce_fusion.1 = f32[128,2048]{1,0:T(8,128)S(1)} fusion(f32[128,16]{1,0:T(8,128)S(1)} %copy.93, f32[2048]{0:T(1024)S(1)} %iota_convert_fusion, f32[128,16]{1,0:T(8,128)S(1)} %copy.49), kind=kLoop, calls=%fused_computation.1 | loop fusion | flops 12320768 | bytes 1073152
  52.5 1.3 copy.69
  54.1 6.6 %all-to-all-done.3 = bf16[16,128,128]{2,1,0:T(8,128)(2,1)S(1)} async-done(((bf16[16,128,128]{2,1,0:T(8,128)(2,1)}), bf16[16,128,128]{2,1,0:T(8,128)(2,1)S(1)}, u32[]{:S(2)}, u32[]{:S(2)}) %all-to-all-start.3) | async-done | bytes 524320 | tf_op jit(solution)/shard_map/all_to_all | solution.py:146
  60.8 4.4 %all-to-all-start = ((bf16[16,128,128]{2,1,0:T(8,128)(2,1)}), bf16[16,128,128]{2,1,0:T(8,128)(2,1)}, u32[]{:S(2)}, u32[]{:S(2)}) async-start(bf16[16,128,128]{2,1,0:T(8,128)(2,1)} %bitcast.1), calls=%async_computation | async-start | bytes 1048576 | tf_op jit(solution)/shard_map/all_to_all | solution.py:149
  65.8 1.5 convert_bitcast_fusion.1
  67.7 1.5 convert_bitcast_fusion
  69.2 1.3 copy.50
  70.5 8.6 %all-to-all-done = bf16[16,128,128]{2,1,0:T(8,128)(2,1)} async-done(((bf16[16,128,128]{2,1,0:T(8,128)(2,1)}), bf16[16,128,128]{2,1,0:T(8,128)(2,1)}, u32[]{:S(2)}, u32[]{:S(2)}) %all-to-all-start) | async-done | bytes 524320 | tf_op jit(solution)/shard_map/all_to_all | solution.py:149
  79.1 2.1 convert_bitcast_fusion.3
  81.3 1.6 copy.46
  82.8 2.0 fusion.33
  85.3 14.2 %fusion.17 = f32[384,2,64,64]{0,2,3,1:T(8,128)S(1)} fusion(f32[384,64,64]{0,2,1:T(8,128)S(1)} %bitcast.170, f32[1,64,64]{1,2,0:T(8,128)S(1)} %get-tuple-element.34, f32[1,64,64]{1,2,0:T(8,128)S(1)} %get-tuple-element.35), kind=kOutput, calls=%fused_computation.33 | convolution fusion | flops 2415927296 | bytes 18907136 | tf_op jit(solution)/shard_map/cab,pak->cpkb/dot_general | solution.py:32
  99.5 3.7 multiply_subtract_fusion.1
  103.3 9.6 %pad_maximum_fusion = f32[384,2,64,64]{0,2,3,1:T(8,128)} fusion(f32[384,1,64,64]{0,2,3,1:T(8,128)} %get-tuple-element.12, f32[384,1,64,64]{0,2,3,1:T(8,128)S(1)} %get-tuple-element.11), kind=kLoop, calls=%fused_computation.4 | loop fusion | flops 3145728 | bytes 25165824 | tf_op jit(solution)/shard_map/stack | solution.py:35
  112.9 22.9 %fusion.20 = f32[384,2,64,64]{0,3,2,1:T(8,128)S(1)} fusion(f32[384,2,64,64]{0,2,3,1:T(8,128)} %pad_maximum_fusion, f32[1,2,64,64]{2,3,1,0:T(8,128)S(1)} %get-tuple-element.25, f32[1,2,64,64]{2,3,1,0:T(8,128)S(1)} %get-tuple-element.28), kind=kOutput, calls=%fused_computation.34 | convolution fusion | flops 4831854592 | bytes 25231360 | tf_op jit(solution)/shard_map/cpkb,pqbm->cqkm/dot_general | solution.py:42
  135.8 2.8 subtract_bitcast_fusion.1
  138.5 4.3 %subtract_bitcast_fusion.2 = (f32[128,64,64]{0,2,1:T(8,128)}, f32[128,64,64]{0,2,1:T(8,128)}, f32[128,64,64]{0,2,1:T(8,128)}, f32[128,64,64]{0,2,1:T(8,128)}) fusion(f32[384,2,64,64]{0,3,2,1:T(8,128)S(1)} %fusion.20), kind=kLoop, calls=%fused_computation.41 | loop fusion | flops 6291456 | bytes 20971520 | tf_op jit(solution)/shard_map/sub | solution.py:88
  142.8 3.7 maximum_bitcast_fusion.1
  148.2 13.8 %fusion.23 = f32[2,64,384,64]{2,1,3,0:T(8,128)} fusion(f32[384,1,64,64]{0,3,2,1:T(8,128)S(1)} %maximum_bitcast_fusion.1, f32[384,1,64,64]{0,3,2,1:T(8,128)S(1)} %maximum_bitcast_fusion, f32[1,2,64,64]{2,3,1,0:T(8,128)S(1)} %get-tuple-element.29, f32[1,2,64,64]{2,3,1,0:T(8,128)S(1)} %get-tuple-element.24), kind=kOutput, calls=%fused_computation.35 | convolution fusion | flops 4835000320 | bytes 25231360 | tf_op jit(solution)/shard_map/cpkm,pqbm->cqkb/dot_general | solution.py:48
  162.0 16.4 %copy.121 = f32[2,64,384,64]{2,3,1,0:T(8,128)} copy(f32[2,64,384,64]{2,1,3,0:T(8,128)} %fusion.23) | data formatting | bytes 25165824 | tf_op jit(solution)/shard_map/cpkm,pqbm->cqkb/dot_general | solution.py:48
  178.4 6.0 %multiply_add_fusion = (f32[384,1,64,64]{0,2,3,1:T(8,128)S(1)}, f32[384,1,64,64]{0,2,3,1:T(8,128)S(1)}) fusion(f32[384,2,64,64]{0,2,3,1:T(8,128)} %bitcast.168, f32[64,64]{0,1:T(8,128)S(1)} %get-tuple-element.36, f32[64,64]{0,1:T(8,128)S(1)} %get-tuple-element.37), kind=kLoop, calls=%fused_computation.30 | loop fusion | flops 9437184 | bytes 25198592 | tf_op jit(solution)/shard_map/add | solution.py:53
  184.3 7.4 %fusion.13 = f32[384,64,64]{0,1,2:T(8,128)S(1)} fusion(f32[384,1,64,64]{0,2,3,1:T(8,128)S(1)} %get-tuple-element.10, f32[384,1,64,64]{0,2,3,1:T(8,128)S(1)} %get-tuple-element.9, f32[1,64,64]{1,2,0:T(8,128)S(1)} %get-tuple-element.34, f32[1,64,64]{1,2,0:T(8,128)S(1)} %get-tuple-element.35), kind=kOutput, calls=%fused_computation.23 | convolution fusion | flops 2420645888 | bytes 18907136 | tf_op jit(solution)/shard_map/cpkb,pak->cab/dot_general | solution.py:58
  191.8 3.6 copy.59
  196.2 1.2 copy-done.4
  197.4 1.1 copy-done.6
  199.8 8.5 %copy.124 = bf16[1,128,2048]{1,0,2:T(2,128)(2,1)S(1)} copy(bf16[1,128,2048]{1,2,0:T(8,128)(2,1)S(1)} %bitcast.182) | data formatting | bytes 1048576 | tf_op jit(solution)/shard_map/reshape | solution.py:143
  208.9 11.5 %reduce.4 = bf16[2048,128]{1,0:T(8,128)(2,1)S(1)} reduce(bf16[2048,1,128]{2,1,0:T(2,128)(2,1)S(1)} %bitcast.174, bf16[]{:T(256)} %broadcast.254), dimensions={1}, to_apply=%bitcast.167.reduce_sub_computation | reduce | bytes 1048578
  221.3 4.0 all-to-all-start.4
  225.4 8.1 %copy.123 = bf16[1,128,2048]{1,0,2:T(2,128)(2,1)S(1)} copy(bf16[1,128,2048]{1,2,0:T(8,128)(2,1)S(1)} %bitcast.181) | data formatting | bytes 1048576 | tf_op jit(solution)/shard_map/reshape | solution.py:143
  233.5 11.5 %reduce.5 = bf16[2048,128]{1,0:T(8,128)(2,1)S(1)} reduce(bf16[2048,1,128]{2,1,0:T(2,128)(2,1)S(1)} %bitcast.176, bf16[]{:T(256)} %broadcast.254), dimensions={1}, to_apply=%bitcast.166.reduce_sub_computation | reduce | bytes 1048578
  246.0 8.3 %copy.122 = bf16[1,128,2048]{1,0,2:T(2,128)(2,1)S(1)} copy(bf16[1,128,2048]{1,2,0:T(8,128)(2,1)S(1)} %bitcast.180) | data formatting | bytes 1048576 | tf_op jit(solution)/shard_map/reshape | solution.py:143
  254.3 11.5 %reduce.6 = bf16[2048,128]{1,0:T(8,128)(2,1)S(1)} reduce(bf16[2048,1,128]{2,1,0:T(2,128)(2,1)S(1)} %bitcast.175, bf16[]{:T(256)} %broadcast.254), dimensions={1}, to_apply=%bitcast.165.reduce_sub_computation | reduce | bytes 1048578
  266.8 7.0 %all-to-all-start.5 = ((bf16[16,2,8192]{2,1,0:T(2,128)(2,1)}), bf16[16,2,8192]{2,1,0:T(2,128)(2,1)S(1)}, u32[]{:S(2)}, u32[]{:S(2)}) async-start(bf16[16,2,8192]{2,1,0:T(2,128)(2,1)} %reshape.265), calls=%async_computation.5 | async-start | bytes 1048576 | tf_op jit(solution)/shard_map/all_to_all | solution.py:163
  273.8 1.6 slice_multiply_fusion
  275.3 2.0 copy.77
  277.6 3.3 multiply_reduce_fusion
  281.0 6.4 %all-to-all-done.5 = bf16[16,2,8192]{2,1,0:T(2,128)(2,1)S(1)} async-done(((bf16[16,2,8192]{2,1,0:T(2,128)(2,1)}), bf16[16,2,8192]{2,1,0:T(2,128)(2,1)S(1)}, u32[]{:S(2)}, u32[]{:S(2)}) %all-to-all-start.5) | async-done | bytes 524320 | tf_op jit(solution)/shard_map/all_to_all | solution.py:163
  287.4 3.8 all-to-all-start.6
  291.2 34.5 %fusion = f32[128,1,16]{2,1,0:T(1,128)S(1)} fusion(f32[128,2048,1]{1,2,0:T(1,128)S(1)} %copy-done.15, f32[2048]{0:T(1024)S(1)} %iota_convert_fusion, f32[128,16]{1,0:T(8,128)S(1)} %copy-done.17), kind=kOutput, calls=%fused_computation.3 | convolution fusion | flops 54525952 | bytes 1073152 | tf_op jit(solution)/shard_map/ct,cmt->cm/dot_general | solution.py:106
  326.3 3.3 all-reduce.2
  329.6 77.1 %all-reduce.1 = (f32[64,16]{0,1:T(8,128)S(1)}, f32[64,16]{0,1:T(8,128)S(1)}) all-reduce(f32[64,16]{0,1:T(8,128)S(1)} %get-tuple-element.7, f32[64,16]{0,1:T(8,128)S(1)} %get-tuple-element.8), channel_id=1, replica_groups=mesh['ctx'=16,'tp'=2] {'ctx'}, use_global_device_ids=true, to_apply=%region_1.2 | all-reduce | flops 2048 | bytes 16384 | tf_op jit(solution)/shard_map/psum | solution.py:171
  408.6 1.0 copy.61
  410.2 1.0 copy.63
  411.9 1.0 copy.65
  (75 shorter events, 14.6 us)
Async XLA Ops:
  0.6 45.7 %copy-start = (f32[64,16]{0,1:T(8,128)S(1)}, f32[64,16]{0,1:T(8,128)}, u32[]{:S(2)}) copy-start(f32[64,16]{0,1:T(8,128)} %param.11) | copy-start | bytes 12292
  24.1 18.4 %all-to-all-start.2 = ((bf16[16,128,128]{2,1,0:T(8,128)(2,1)}), bf16[16,128,128]{2,1,0:T(8,128)(2,1)S(1)}, u32[]{:S(2)}, u32[]{:S(2)}) async-start(bf16[16,128,128]{2,1,0:T(8,128)(2,1)} %bitcast.184), calls=%async_computation.2 | async-start | bytes 1048576 | tf_op jit(solution)/shard_map/all_to_all | solution.py:148
  28.1 37.3 %copy-start.18 = (s32[128]{0:T(128)}, s32[128]{0:T(128)S(1)}, u32[]{:S(2)}) copy-start(s32[128]{0:T(128)S(1)} %and_select_fusion) | copy-start | bytes 1540
  42.5 22.9 %copy-start.13 = (bf16[16,128,128]{2,1,0:T(8,128)(2,1)}, bf16[16,128,128]{2,1,0:T(8,128)(2,1)S(1)}, u32[]{:S(2)}) copy-start(bf16[16,128,128]{2,1,0:T(8,128)(2,1)S(1)} %all-to-all-done.2) | copy-start | bytes 1572868
  42.5 18.3 %all-to-all-start.3 = ((bf16[16,128,128]{2,1,0:T(8,128)(2,1)}), bf16[16,128,128]{2,1,0:T(8,128)(2,1)S(1)}, u32[]{:S(2)}, u32[]{:S(2)}) async-start(bf16[16,128,128]{2,1,0:T(8,128)(2,1)} %bitcast.185), calls=%async_computation.3 | async-start | bytes 1048576 | tf_op jit(solution)/shard_map/all_to_all | solution.py:146
  47.3 18.2 %copy-start.16 = (f32[128,16]{1,0:T(8,128)}, f32[128,16]{1,0:T(8,128)S(1)}, u32[]{:S(2)}) copy-start(f32[128,16]{1,0:T(8,128)S(1)} %copy.49) | copy-start | bytes 24580
  60.8 4.6 %copy-start.14 = (bf16[16,128,128]{2,1,0:T(8,128)(2,1)}, bf16[16,128,128]{2,1,0:T(8,128)(2,1)S(1)}, u32[]{:S(2)}) copy-start(bf16[16,128,128]{2,1,0:T(8,128)(2,1)S(1)} %all-to-all-done.3) | copy-start | bytes 1572868
  60.8 18.4 %all-to-all-start = ((bf16[16,128,128]{2,1,0:T(8,128)(2,1)}), bf16[16,128,128]{2,1,0:T(8,128)(2,1)}, u32[]{:S(2)}, u32[]{:S(2)}) async-start(bf16[16,128,128]{2,1,0:T(8,128)(2,1)} %bitcast.1), calls=%async_computation | async-start | bytes 1048576 | tf_op jit(solution)/shard_map/all_to_all | solution.py:149
  65.8 19.0 %copy-start.3 = (f32[1,128,16,128]{1,3,2,0:T(8,128)}, f32[1,128,16,128]{1,3,2,0:T(8,128)S(1)}, u32[]{:S(2)}) copy-start(f32[1,128,16,128]{1,3,2,0:T(8,128)S(1)} %copy.47) | copy-start | bytes 3145732
  67.7 17.2 %copy-start.5 = (f32[1,128,16,128]{1,3,2,0:T(8,128)}, f32[1,128,16,128]{1,3,2,0:T(8,128)S(1)}, u32[]{:S(2)}) copy-start(f32[1,128,16,128]{1,3,2,0:T(8,128)S(1)} %copy.48) | copy-start | bytes 3145732
  82.8 2.5 copy-start.7
  82.8 2.1 copy-start.12
  142.8 3.7 copy-start.9
  142.8 4.1 copy-start.10
  142.8 4.7 %copy-start.11 = (f32[128,64,64]{0,2,1:T(8,128)S(1)}, f32[128,64,64]{0,2,1:T(8,128)}, u32[]{:S(2)}) copy-start(f32[128,64,64]{0,2,1:T(8,128)} %get-tuple-element.15) | copy-start | bytes 6291460
  195.4 4.4 %copy-start.2 = (f32[384,64,64]{0,2,1:T(8,128)}, f32[384,64,64]{0,2,1:T(8,128)S(1)}, u32[]{:S(2)}) copy-start(f32[384,64,64]{0,2,1:T(8,128)S(1)} %copy.59) | copy-start | bytes 18874372
  195.4 2.0 copy-start.4
  195.4 3.1 copy-start.6
  195.4 4.1 copy-start.8
  221.3 45.4 %all-to-all-start.4 = ((bf16[16,2,8192]{2,1,0:T(2,128)(2,1)}), bf16[16,2,8192]{2,1,0:T(2,128)(2,1)S(1)}, u32[]{:S(2)}, u32[]{:S(2)}) async-start(bf16[16,2,8192]{2,1,0:T(2,128)(2,1)} %reshape.263), calls=%async_computation.4 | async-start | bytes 1048576 | tf_op jit(solution)/shard_map/all_to_all | solution.py:162
  246.0 31.7 %copy-start.17 = (f32[128,16]{1,0:T(8,128)S(1)}, f32[128,16]{1,0:T(8,128)}, u32[]{:S(2)}) copy-start(f32[128,16]{1,0:T(8,128)} %copy-done.16) | copy-start | bytes 24580
  266.8 20.6 %all-to-all-start.5 = ((bf16[16,2,8192]{2,1,0:T(2,128)(2,1)}), bf16[16,2,8192]{2,1,0:T(2,128)(2,1)S(1)}, u32[]{:S(2)}, u32[]{:S(2)}) async-start(bf16[16,2,8192]{2,1,0:T(2,128)(2,1)} %reshape.265), calls=%async_computation.5 | async-start | bytes 1048576 | tf_op jit(solution)/shard_map/all_to_all | solution.py:163
  277.6 13.6 %copy-start.15 = (f32[128,2048,1]{1,2,0:T(1,128)S(1)}, f32[128,2048,1]{1,2,0:T(1,128)}, u32[]{:S(2)}) copy-start(f32[128,2048,1]{1,2,0:T(1,128)} %copy.77) | copy-start | bytes 3145732
  287.4 123.9 %all-to-all-start.6 = ((bf16[16,2,8192]{2,1,0:T(2,128)(2,1)}), bf16[16,2,8192]{2,1,0:T(2,128)(2,1)S(1)}, u32[]{:S(2)}, u32[]{:S(2)}) async-start(bf16[16,2,8192]{2,1,0:T(2,128)(2,1)} %reshape.267), calls=%async_computation.6 | async-start | bytes 1048576 | tf_op jit(solution)/shard_map/all_to_all | solution.py:164
  291.2 34.6 %copy-start.19 = (s32[128]{0:T(128)S(1)}, s32[128]{0:T(128)}, u32[]{:S(2)}) copy-start(s32[128]{0:T(128)} %copy-done.18) | copy-start | bytes 1540
  291.2 34.6 %copy-start.20 = (f32[128,16]{0,1:T(8,128)S(1)}, f32[128,16]{0,1:T(8,128)}, u32[]{:S(2)}) copy-start(f32[128,16]{0,1:T(8,128)} %get-tuple-element.31) | copy-start | bytes 24580
  407.4 5.5 %copy-start.1 = (f32[64,16]{0,1:T(8,128)S(1)}, f32[64,16]{0,1:T(8,128)}, u32[]{:S(2)}) copy-start(f32[64,16]{0,1:T(8,128)} %param.11) | copy-start | bytes 12292
